TPU v7x, 32 devices: a whole 2x2x4 slice. The times are simulated.
32 devices in a mesh: boot: 4 (over z), tm: 8 (over y, x, core).
Axes of the slice: x: 2, y: 2, z: 4, core: 2. Of those that a mesh axis runs over, the one named last changes fastest.
Arguments:
- recording: bfloat16 [4096, 1024], P('tm'), may hold values from -60 to 60, as said below
- starts: int32 [4, 48], P('boot', 'tm'), may hold values from 0 to 448, as said below
- lengths: int32 [4, 48], P('boot', 'tm'), may hold values from 1 to 64, as said below
- support: int32 [4, 4096], P(None, 'boot'), may hold values 0 or 1
Outputs:
- averaged: float32 [32, 4096], P(None, 'boot')
- residual: float32 [32, 4096], P(None, 'tm')
Inputs may be any that keep to these rules, and one draw needn't show every extreme that they name: A shard's values are an autoregressive recording; its values stay within the range. Entry [b, j * 6 + k] starts block k of resample b on time shard j, counted from the shard's first sample; a block ends inside its shard. The 6 lengths of one resample on one time shard sum to at most 384.
All inputs are finite; a program needn't handle non-finite values. No bound on the sum of `support` on one device may be relied on, other than what follows from the above.
Results may differ from a plain program's by a relative error of at most 0.0043.
The roundings to bfloat16 on the way count: a program that leaves them out, or rounds other values in their place, can miss the bound.
Values may be sent and summed in bfloat16 or wider, within the bound.
No kernel may reach another device: no remote copies, remote signals or barrier semaphores. Data moves between devices by JAX's collectives and lax.ppermute only.
A program may use at most 64 MiB of HBM per device.

v0:
```python
import jax
import jax.numpy as jnp
from jax import lax
from jax.sharding import PartitionSpec as P

CHANNEL_COUNT = 1024
LAGS = 4
RESPONSE_COUNT = 32
NBLK = 6
CAP = 384
ITERS = 3
CHEB = 5
ridge_weight = 4.0
shrink_level = 0.75
epsilon = 1e-05


def passed_along(block, axis, distance):
    devices = range(lax.axis_size(axis))
    route = [(i - distance, i) for i in devices if i - distance in devices]
    return lax.ppermute(block, axis, route)


def bootstrap_rows(window, begins, sizes):
    ends = jnp.cumsum(sizes)
    offsets = ends - sizes
    total = ends[-1]
    rows = jnp.arange(CAP, dtype=jnp.int32)
    member = (rows[:, None] >= offsets[None, :]).astype(jnp.int32)
    which = jnp.sum(member, axis=1) - 1
    picked = (which[:, None] == jnp.arange(NBLK, dtype=jnp.int32)[None, :]).astype(jnp.int32)
    anchor = jnp.sum(picked * offsets[None, :], axis=1)
    opening = jnp.sum(picked * begins[None, :], axis=1)
    live = rows < total
    times = jnp.where(live, opening + rows - anchor, 0)
    blocks = [jnp.take(window, times + LAGS - 1 - delay_step, axis=0) for delay_step in range(LAGS)]
    design = jnp.concatenate(blocks, axis=1)
    design = jnp.where(live[:, None], design, jnp.zeros_like(design))
    answer = jnp.take(window[:, :RESPONSE_COUNT], times + LAGS, axis=0)
    answer = jnp.where(live[:, None], answer, jnp.zeros_like(answer))
    return (design, answer.T)


def chebyshev(gram, rhs, bound):
    center = ridge_weight + 0.5 * bound
    radius = 0.5 * bound
    sigma = center / radius
    solution = jnp.zeros_like(rhs)
    remain = rhs
    factor = 1.0 / sigma
    update = rhs / center
    for count in range(CHEB):
        solution = solution + update
        if count + 1 < CHEB:
            applied = ridge_weight * update + jnp.einsum(
                "brc,bcd->brd", update, gram, precision=lax.Precision.HIGHEST
            )
            remain = remain - applied
            after = 1.0 / (2.0 * sigma - factor)
            update = after * factor * update + 2.0 * after / radius * remain
            factor = after
    return solution


def shrink_columns(mean_value, norms, level):
    return mean_value * (jnp.maximum(norms - level, 0.0) / jnp.maximum(norms, level))[:, None, :]


def per_device(recording, starts, lengths, support):
    shards = lax.axis_size("tm")
    samples = recording.shape[0]
    values = recording.astype(jnp.float32)
    power = lax.psum(jnp.sum(values * values, axis=0), "tm")
    scale = 1.0 / jnp.sqrt(power / (samples * shards) + epsilon)
    scaled_input = (values * scale).astype(jnp.bfloat16)
    carried = passed_along(scaled_input[samples - LAGS :], "tm", 1)
    extended = jnp.concatenate([carried, scaled_input], axis=0)
    design, answer = jax.vmap(bootstrap_rows, in_axes=(None, 0, 0))(extended, starts, lengths)
    row_scale = 1.0 / CAP
    cross = (
        jnp.einsum("brc,bcf->brf", answer, design, preferred_element_type=jnp.float32) * row_scale
    )
    gram = (
        jnp.einsum("bcf,bdf->bcd", design, design, preferred_element_type=jnp.float32) * row_scale
    )
    bound = jnp.sqrt(jnp.sum(gram * gram, axis=(1, 2)))[:, None, None]
    consensus = jnp.zeros_like(cross)
    dual = jnp.zeros_like(cross)
    for rounds in range(ITERS):
        target = cross + ridge_weight * (consensus - dual)
        projected = (
            jnp.einsum(
                "brf,bcf->brc",
                target.astype(jnp.bfloat16),
                design,
                preferred_element_type=jnp.float32,
            )
            * row_scale
        )
        weights = chebyshev(gram, projected, bound)
        back = jnp.einsum(
            "brc,bcf->brf", weights.astype(jnp.bfloat16), design, preferred_element_type=jnp.float32
        )
        local = (target - back) / ridge_weight
        stacked = local + dual
        mean_value = lax.psum(stacked, "tm") / shards
        norms = jnp.sqrt(jnp.sum(mean_value * mean_value, axis=1))
        level = shrink_level * jnp.mean(norms, axis=1, keepdims=True)
        consensus = shrink_columns(mean_value, norms, level)
        dual = dual + local - consensus
    width = consensus.shape[2] // lax.axis_size("boot")
    position = lax.axis_index("boot")
    chosen = support.astype(jnp.float32)
    tally = jnp.sum(chosen, axis=0)
    mine = lax.all_to_all(support, "boot", split_axis=0, concat_axis=1, tiled=True).astype(
        jnp.float32
    )
    weighted = jnp.sum(mine[:, None, :] * consensus, axis=0)
    summed = lax.psum_scatter(weighted, "boot", scatter_dimension=1, tiled=True)
    averaged = summed / jnp.maximum(tally, 1.0)[None, :]
    opening = position * width
    delay_step = opening // CHANNEL_COUNT
    channel = opening % CHANNEL_COUNT
    columns = lax.dynamic_slice(extended, (LAGS - 1 - delay_step, channel), (samples, width))
    partial_result = lax.dot_general(
        averaged.astype(jnp.bfloat16),
        columns,
        (((1,), (1,)), ((), ())),
        preferred_element_type=jnp.float32,
    )
    predicted_output = lax.psum(partial_result, "boot")
    residual = scaled_input[:, :RESPONSE_COUNT].astype(jnp.float32).T - predicted_output
    return (averaged, residual)


def solution(mesh):
    in_specs = (P("tm", None), P("boot", "tm"), P("boot", "tm"), P(None, "boot"))
    out_specs = (P(None, "boot"), P(None, "tm"))
    return jax.shard_map(
        per_device, mesh=mesh, in_specs=in_specs, out_specs=out_specs, check_vma=False
    )
```

profile of v0, /device:TPU:0, one launch (start us, length us, event | category | flops | bytes accessed | tf_op | source)
XLA Modules:
  0.0 315.7 jit_solution(589085711330140276)
XLA Ops:
  7.2 1.5 copy.24
  9.0 15.2 %psum.35 = f32[1024]{0:T(1024)S(1)} all-reduce(f32[1024]{0:T(1024)S(1)} %fusion.9), channel_id=1, replica_groups=mesh['boot'=4,'tm'=8] {'tm'}, use_global_device_ids=true, to_apply=%region_5.6 | all-reduce | flops 1024 | bytes 8192 | tf_op jit(solution)/shard_map/psum | solution.py:73
  24.6 1.3 collective-permute-start
  26.1 0.6 slice.12
  26.9 0.7 iota_compare_fusion
  27.6 0.7 fusion.114
  28.3 0.7 and_reduce_fusion.3
  29.1 0.7 copy-done.10
  29.8 0.7 pad_maximum_fusion
  30.5 0.6 copy.26
  31.1 2.7 gather_fusion.4
  33.8 2.7 gather_fusion.3
  36.5 2.7 gather_fusion.2
  39.2 2.7 gather_fusion.1
  41.9 2.7 fusion.38
  44.5 1.4 fusion.42
  45.9 0.9 fusion.8
  46.8 2.5 multiply_reduce_fusion
  50.7 1.4 gather_fusion
  52.1 2.7 convolution_multiply_fusion
  54.8 2.1 maximum_select_fusion.1
  56.9 1.0 convolution_multiply_fusion.4
  58.8 0.4 fusion.29
  59.3 0.4 fusion.32
  59.7 1.5 fusion.1
  61.5 58.2 %all-reduce.5.cloned.1.call-done = f32[1,32,4096]{2,1,0:T(8,128)} async-done(((f32[1,32,4096]{2,1,0:T(8,128)}), f32[1,32,4096]{2,1,0:T(8,128)}) %all-reduce.5.cloned.1.call-update) | async-done | bytes 524304 | tf_op jit(solution)/shard_map/psum | solution.py:106
  119.7 1.1 multiply_reduce_fusion.3
  120.8 0.7 sqrt_reduce_fusion.2
  122.1 3.4 %convolution_multiply_fusion.3 = f32[32,384]{1,0:T(8,128)S(1)} fusion(bf16[384,4096]{1,0:T(8,128)(2,1)} %copy-done.3, f32[1,32,4096]{2,1,0:T(8,128)} %fusion.1, f32[1,32,4096]{2,1,0:T(8,128)} %all-reduce.5.cloned.1.call-done, f32[32,4096]{1,0:T(8,128)S(1)} %convolution_multiply_fusion, f32[4096]{0:T(1024)S(1)} %divide_multiply_fusion.2), kind=kOutput, calls=%fused_computation.31 | convolution fusion | flops 101462016 | bytes 4784128 | tf_op jit(solution)/shard_map/brf,bcf->brc/dot_general | solution.py:92
  126.8 0.4 fusion.33
  127.3 1.5 fusion.7
  129.0 54.2 %all-reduce.7.cloned.1.call-done = f32[1,32,4096]{2,1,0:T(8,128)} async-done(((f32[1,32,4096]{2,1,0:T(8,128)}), f32[1,32,4096]{2,1,0:T(8,128)}) %all-reduce.7.cloned.1.call-update) | async-done | bytes 524304 | tf_op jit(solution)/shard_map/psum | solution.py:106
  183.2 1.1 multiply_reduce_fusion.2
  184.3 0.7 sqrt_reduce_fusion.1
  185.6 3.4 %convolution_multiply_fusion.2 = f32[32,384]{1,0:T(8,128)S(1)} fusion(bf16[384,4096]{1,0:T(8,128)(2,1)} %copy-done.3, f32[1,32,4096]{2,1,0:T(8,128)} %fusion.7, f32[1,32,4096]{2,1,0:T(8,128)} %all-reduce.7.cloned.1.call-done, f32[32,4096]{1,0:T(8,128)S(1)} %convolution_multiply_fusion, f32[4096]{0:T(1024)S(1)} %divide_multiply_fusion.1), kind=kOutput, calls=%fused_computation.30 | convolution fusion | flops 101462016 | bytes 4784128 | tf_op jit(solution)/shard_map/brf,bcf->brc/dot_general | solution.py:92
  189.9 0.4 fusion.15
  190.4 0.4 fusion.34
  190.9 1.5 fusion.4
  192.5 9.9 %all_to_all.13 = s32[4,1,1024]{2,1,0:T(1,128)S(1)} all-to-all(s32[4,1,1024]{2,1,0:T(1,128)S(1)} %all_to_all.10), channel_id=1, replica_groups=mesh['boot'=4,'tm'=8] {'boot'}, dimensions={0} | all-to-all | bytes 32768 | tf_op jit(solution)/shard_map/all_to_all | solution.py:115
  202.5 44.2 %all-reduce.9.cloned.1.call-done = f32[1,32,4096]{2,1,0:T(8,128)} async-done(((f32[1,32,4096]{2,1,0:T(8,128)}), f32[1,32,4096]{2,1,0:T(8,128)}) %all-reduce.9.cloned.1.call-update) | async-done | bytes 524304 | tf_op jit(solution)/shard_map/psum | solution.py:106
  246.7 1.1 multiply_reduce_fusion.1
  247.8 0.6 sqrt_reduce_fusion
  249.1 1.9 multiply_bitcast_fusion
  251.1 21.2 %reduce-scatter.2.cloned.1.call-done = f32[32,1024]{1,0:T(8,128)} async-done(((f32[32,4096]{1,0:T(8,128)}), f32[32,1024]{1,0:T(8,128)}) %reduce-scatter.2.cloned.1.call-update) | async-done | bytes 131088 | tf_op jit(solution)/shard_map/reduce_scatter | solution.py:119
  272.4 0.9 broadcast_divide_fusion
  273.3 1.3 fusion.36
  274.6 33.1 %all-reduce.11.cloned.1.call-done = f32[32,512]{1,0:T(8,128)} async-done(((f32[32,512]{1,0:T(8,128)}), f32[32,512]{1,0:T(8,128)}) %all-reduce.11.cloned.1.call-update) | async-done | bytes 65552 | tf_op jit(solution)/shard_map/psum | solution.py:131
  307.7 1.5 bitcast_subtract_fusion
  (73 shorter events, 5.0 us)
Async XLA Ops:
  7.2 18.8 %copy-start.15 = (s32[1,6]{1,0:T(1,128)S(1)}, s32[1,6]{1,0:T(1,128)}, u32[]{:S(2)}) copy-start(s32[1,6]{1,0:T(1,128)} %param.8) | copy-start | bytes 76
  7.2 19.6 %copy-start.14 = (s32[1,6]{1,0:T(1,128)S(1)}, s32[1,6]{1,0:T(1,128)}, u32[]{:S(2)}) copy-start(s32[1,6]{1,0:T(1,128)} %param.7) | copy-start | bytes 76
  7.2 112.5 %all-reduce.5.cloned.1.call-start = ((), (), s32[]{:S(2)}) async-start(), calls=%async_computation.2 | async-start | bytes 1048576 | tf_op jit(solution)/shard_map/psum | solution.py:106
  24.6 4.4 %collective-permute-start = (bf16[4,1024]{0,1:T(8,128)(2,1)S(1)}, bf16[4,1024]{0,1:T(8,128)(2,1)S(1)}, u32[]{:S(2)}, u32[]{:S(2)}) collective-permute-start(bf16[4,1024]{0,1:T(8,128)(2,1)S(1)} %slice.26), channel_id=1, source_target_pairs={{0,1},{1,2},{2,3},{3,4},{4,5},{5,6},{6,7},{8,9},{9,10},{10,11},{11... | collective-permute-start | bytes 24584 | tf_op jit(solution)/shard_map/ppermute | solution.py:21
  29.1 0.7 copy-start.10
  41.9 2.7 copy-start.8
  41.9 2.7 copy-start.9
  46.8 2.5 copy-start.3
  46.8 3.4 %copy-start.11 = (bf16[4,1024]{0,1:T(8,128)(2,1)S(1)}, bf16[4,1024]{0,1:T(8,128)(2,1)}, u32[]{:S(2)}) copy-start(bf16[4,1024]{0,1:T(8,128)(2,1)} %copy-done.10) | copy-start | bytes 24580
  56.9 2.8 copy-start
  61.3 121.9 %all-reduce.7.cloned.1.call-start = ((), (), s32[]{:S(2)}) async-start(), calls=%async_computation.3 | async-start | bytes 1048576 | tf_op jit(solution)/shard_map/psum | solution.py:106
  122.1 5.2 %copy-start.1 = (bf16[384,4096]{1,0:T(8,128)(2,1)S(1)}, bf16[384,4096]{1,0:T(8,128)(2,1)}, u32[]{:S(2)}) copy-start(bf16[384,4096]{1,0:T(8,128)(2,1)} %copy-done) | copy-start | bytes 9437188
  122.1 5.2 %copy-start.5 = (f32[1,32,4096]{2,1,0:T(8,128)S(1)}, f32[1,32,4096]{2,1,0:T(8,128)}, u32[]{:S(2)}) copy-start(f32[1,32,4096]{2,1,0:T(8,128)} %fusion.1) | copy-start | bytes 1572868
  122.1 5.2 %copy-start.7 = (f32[1,32,4096]{2,1,0:T(8,128)S(1)}, f32[1,32,4096]{2,1,0:T(8,128)}, u32[]{:S(2)}) copy-start(f32[1,32,4096]{2,1,0:T(8,128)} %all-reduce.5.cloned.1.call-done) | copy-start | bytes 1572868
  128.9 117.8 %all-reduce.9.cloned.1.call-start = ((), (), s32[]{:S(2)}) async-start(), calls=%async_computation.4 | async-start | bytes 1048576 | tf_op jit(solution)/shard_map/psum | solution.py:106
  185.6 5.2 %copy-start.2 = (bf16[384,4096]{1,0:T(8,128)(2,1)S(1)}, bf16[384,4096]{1,0:T(8,128)(2,1)}, u32[]{:S(2)}) copy-start(bf16[384,4096]{1,0:T(8,128)(2,1)} %copy-done) | copy-start | bytes 9437188
  185.6 5.2 %copy-start.4 = (f32[1,32,4096]{2,1,0:T(8,128)S(1)}, f32[1,32,4096]{2,1,0:T(8,128)}, u32[]{:S(2)}) copy-start(f32[1,32,4096]{2,1,0:T(8,128)} %fusion.7) | copy-start | bytes 1572868
  185.6 5.2 %copy-start.6 = (f32[1,32,4096]{2,1,0:T(8,128)S(1)}, f32[1,32,4096]{2,1,0:T(8,128)}, u32[]{:S(2)}) copy-start(f32[1,32,4096]{2,1,0:T(8,128)} %all-reduce.7.cloned.1.call-done) | copy-start | bytes 1572868
  190.4 2.1 copy-start.13
  192.4 79.9 %reduce-scatter.2.cloned.1.call-start = ((), (), s32[]{:S(2)}) async-start(), calls=%async_computation.5 | async-start | bytes 655360 | tf_op jit(solution)/shard_map/reduce_scatter | solution.py:119
  251.0 56.6 %all-reduce.11.cloned.1.call-start = ((), (), s32[]{:S(2)}) async-start(), calls=%async_computation.6 | async-start | bytes 131072 | tf_op jit(solution)/shard_map/psum | solution.py:131
  273.3 35.9 %copy-start.12 = (f32[32,1024]{1,0:T(8,128)}, f32[32,1024]{1,0:T(8,128)S(1)}, u32[]{:S(2)}) copy-start(f32[32,1024]{1,0:T(8,128)S(1)} %broadcast_divide_fusion) | copy-start | bytes 393220
Sparse Core Ops, SparseCore 0:
  61.4 58.2 all-reduce.4
  129.0 54.1 all-reduce.6
  192.5 54.1 all-reduce.8
  251.2 21.1 reduce-scatter.1
  275.1 32.5 all-reduce.10
where the time goes:
time: 316 us
  waiting for transfers between devices  211 us (67%)
  blocking collectives  25.1 us (8%)
  matrix products  24 us (8%)
  other arithmetic  20.6 us (7%)
  between operations  17.4 us (6%)
  local copies, waits for them, and re-layouts  15.9 us (5%)
    psum x3, waiting for transfers between devices, per_device(): mean_value = lax.psum(stacked, 'tm') / shards  157 us
    psum x1, waiting for transfers between devices, per_device(): predicted_output = lax.psum(partial_result, 'boot')  33.1 us
    reduce_scatter x1, waiting for transfers between devices, per_device(): summed = lax.psum_scatter(weighted, 'boot', scatter_dimension=1, tiled=True)  21.2 us
    psum x1, blocking collectives, per_device(): power = lax.psum(jnp.sum(values * values, axis=0), 'tm')  15.2 us
    gather x4, local copies, waits for them, and re-layouts, bootstrap_rows(): jnp.take(window, times + LAGS - 1 - delay_step, axis=0)  10.8 us
    all_to_all x1, blocking collectives, per_device(): lax.all_to_all(support, 'boot', split_axis=0, concat_axis=1, tiled=True)  9.94 us
    dot_general x3, matrix products, per_device(): jnp.einsum('brf,bcf->brc', target.astype(jnp.bfloat16), design, preferred...  7.84 us
  transfers between devices with their start and end apart: 6, of which 5 were waited for; matrix products, arithmetic and copies ran while one was open for 1% of the time, Pallas kernels for 0%

commit v1 on v0

--- a/solution.py
+++ b/solution.py
@@ -128,7 +128,11 @@
         (((1,), (1,)), ((), ())),
         preferred_element_type=jnp.float32,
     )
-    predicted_output = lax.psum(partial_result, "boot")
+    predicted_output = partial_result
+    for hop in (1, 2):
+        predicted_output = predicted_output + lax.ppermute(
+            predicted_output, "boot", [(dev, dev ^ hop) for dev in range(4)]
+        )
     residual = scaled_input[:, :RESPONSE_COUNT].astype(jnp.float32).T - predicted_output
     return (averaged, residual)
 

time: 316 us -> 291 us (0.921)
  waiting for transfers between devices: 211 us -> 187 us
    psum x1 -> x0, waiting for transfers between devices: 33.1 us -> none  [per_device(): predicted_output = lax.psum(partial_result, 'boot')]
    ppermute x0 -> x2, waiting for transfers between devices: none -> 8.85 us  [per_device(): lax.ppermute(predicted_output, 'boot', [(dev, dev ^ hop) for dev in range...]
  transfers between devices with their start and end apart: 6 -> 7, of which waited for: 5 -> 6; matrix products, arithmetic and copies ran while one was open for 1% -> 1% of each run, Pallas kernels for 0% -> 0%
where the time goes in v1:
time: 291 us
  waiting for transfers between devices  187 us (64%)
  blocking collectives  25.1 us (9%)
  matrix products  23.4 us (8%)
  other arithmetic  19.7 us (7%)
  between operations  17.4 us (6%)
  local copies, waits for them, and re-layouts  15.9 us (5%)
    psum x3, waiting for transfers between devices, per_device(): mean_value = lax.psum(stacked, 'tm') / shards  157 us
    reduce_scatter x1, waiting for transfers between devices, per_device(): summed = lax.psum_scatter(weighted, 'boot', scatter_dimension=1, tiled=True)  21.3 us
    psum x1, blocking collectives, per_device(): power = lax.psum(jnp.sum(values * values, axis=0), 'tm')  15.2 us
    gather x4, local copies, waits for them, and re-layouts, bootstrap_rows(): jnp.take(window, times + LAGS - 1 - delay_step, axis=0)  10.8 us
    all_to_all x1, blocking collectives, per_device(): lax.all_to_all(support, 'boot', split_axis=0, concat_axis=1, tiled=True)  9.94 us
    ppermute x2, waiting for transfers between devices, per_device(): lax.ppermute(predicted_output, 'boot', [(dev, dev ^ hop) for dev in range...  8.85 us
    dot_general x3, matrix products, per_device(): jnp.einsum('brf,bcf->brc', target.astype(jnp.bfloat16), design, preferred...  7.84 us
  transfers between devices with their start and end apart: 7, of which 6 were waited for; matrix products, arithmetic and copies ran while one was open for 1% of the time, Pallas kernels for 0%

profile of v1, /device:TPU:0, one launch (start us, length us, event | category | flops | bytes accessed | tf_op | source)
XLA Modules:
  0.0 290.8 jit_solution(8321471493580207820)
XLA Ops:
  7.2 1.5 copy.24
  9.0 15.2 %psum.28 = f32[1024]{0:T(1024)S(1)} all-reduce(f32[1024]{0:T(1024)S(1)} %fusion.9), channel_id=1, replica_groups=mesh['boot'=4,'tm'=8] {'tm'}, use_global_device_ids=true, to_apply=%region_5.6 | all-reduce | flops 1024 | bytes 8192 | tf_op jit(solution)/shard_map/psum | solution.py:73
  24.6 1.3 collective-permute-start
  26.1 0.6 slice.12
  26.9 0.7 iota_compare_fusion
  27.6 0.7 fusion.114
  28.3 0.7 and_reduce_fusion.3
  29.1 0.7 copy-done.10
  29.8 0.7 pad_maximum_fusion
  30.5 0.6 copy.26
  31.1 2.7 gather_fusion.4
  33.8 2.7 gather_fusion.3
  36.5 2.7 gather_fusion.2
  39.2 2.7 gather_fusion.1
  41.9 2.7 fusion.38
  44.5 1.4 fusion.42
  45.9 0.9 fusion.8
  46.8 2.5 multiply_reduce_fusion
  50.7 1.4 gather_fusion
  52.1 2.7 convolution_multiply_fusion
  54.8 2.1 maximum_select_fusion.1
  56.9 1.0 convolution_multiply_fusion.4
  59.3 0.5 fusion.32
  59.7 1.5 fusion.1
  61.5 58.2 %all-reduce.4.cloned.1.call-done = f32[1,32,4096]{2,1,0:T(8,128)} async-done(((f32[1,32,4096]{2,1,0:T(8,128)}), f32[1,32,4096]{2,1,0:T(8,128)}) %all-reduce.4.cloned.1.call-update) | async-done | bytes 524304 | tf_op jit(solution)/shard_map/psum | solution.py:106
  119.7 1.1 multiply_reduce_fusion.3
  120.8 0.7 sqrt_reduce_fusion.2
  122.2 3.4 %convolution_multiply_fusion.3 = f32[32,384]{1,0:T(8,128)S(1)} fusion(bf16[384,4096]{1,0:T(8,128)(2,1)} %copy-done.3, f32[1,32,4096]{2,1,0:T(8,128)} %fusion.1, f32[1,32,4096]{2,1,0:T(8,128)} %all-reduce.4.cloned.1.call-done, f32[32,4096]{1,0:T(8,128)S(1)} %convolution_multiply_fusion, f32[4096]{0:T(1024)S(1)} %divide_multiply_fusion.2), kind=kOutput, calls=%fused_computation.31 | convolution fusion | flops 101462016 | bytes 4784128 | tf_op jit(solution)/shard_map/brf,bcf->brc/dot_general | solution.py:92
  126.9 0.5 fusion.33
  127.4 1.5 fusion.7
  129.0 54.2 %all-reduce.6.cloned.1.call-done = f32[1,32,4096]{2,1,0:T(8,128)} async-done(((f32[1,32,4096]{2,1,0:T(8,128)}), f32[1,32,4096]{2,1,0:T(8,128)}) %all-reduce.6.cloned.1.call-update) | async-done | bytes 524304 | tf_op jit(solution)/shard_map/psum | solution.py:106
  183.2 1.1 multiply_reduce_fusion.2
  184.3 0.7 sqrt_reduce_fusion.1
  185.7 3.4 %convolution_multiply_fusion.2 = f32[32,384]{1,0:T(8,128)S(1)} fusion(bf16[384,4096]{1,0:T(8,128)(2,1)} %copy-done.3, f32[1,32,4096]{2,1,0:T(8,128)} %fusion.7, f32[1,32,4096]{2,1,0:T(8,128)} %all-reduce.6.cloned.1.call-done, f32[32,4096]{1,0:T(8,128)S(1)} %convolution_multiply_fusion, f32[4096]{0:T(1024)S(1)} %divide_multiply_fusion.1), kind=kOutput, calls=%fused_computation.30 | convolution fusion | flops 101462016 | bytes 4784128 | tf_op jit(solution)/shard_map/brf,bcf->brc/dot_general | solution.py:92
  190.4 0.5 fusion.34
  190.9 1.5 fusion.4
  192.6 9.9 %all_to_all.13 = s32[4,1,1024]{2,1,0:T(1,128)S(1)} all-to-all(s32[4,1,1024]{2,1,0:T(1,128)S(1)} %all_to_all.10), channel_id=1, replica_groups=mesh['boot'=4,'tm'=8] {'boot'}, dimensions={0} | all-to-all | bytes 32768 | tf_op jit(solution)/shard_map/all_to_all | solution.py:115
  202.5 44.2 %all-reduce.8.cloned.1.call-done = f32[1,32,4096]{2,1,0:T(8,128)} async-done(((f32[1,32,4096]{2,1,0:T(8,128)}), f32[1,32,4096]{2,1,0:T(8,128)}) %all-reduce.8.cloned.1.call-update) | async-done | bytes 524304 | tf_op jit(solution)/shard_map/psum | solution.py:106
  246.7 1.1 multiply_reduce_fusion.1
  247.8 0.6 sqrt_reduce_fusion
  249.1 1.9 multiply_bitcast_fusion
  251.1 21.3 %reduce-scatter.2.cloned.1.call-done = f32[32,1024]{1,0:T(8,128)} async-done(((f32[32,4096]{1,0:T(8,128)}), f32[32,1024]{1,0:T(8,128)}) %reduce-scatter.2.cloned.1.call-update) | async-done | bytes 131088 | tf_op jit(solution)/shard_map/reduce_scatter | solution.py:119
  272.4 0.9 broadcast_divide_fusion
  273.3 0.7 fusion.36
  274.0 4.3 %collective-permute-done.1 = f32[32,512]{1,0:T(8,128)S(1)} collective-permute-done((f32[32,512]{1,0:T(8,128)S(1)}, f32[32,512]{1,0:T(8,128)S(1)}, u32[]{:S(2)}, u32[]{:S(2)}) %collective-permute-start.1) | collective-permute-done | bytes 65568 | tf_op jit(solution)/shard_map/ppermute | solution.py:133
  278.3 0.8 collective-permute-start.2
  279.1 4.6 %collective-permute-done.2 = f32[32,512]{1,0:T(8,128)S(1)} collective-permute-done((f32[32,512]{1,0:T(8,128)S(1)}, f32[32,512]{1,0:T(8,128)S(1)}, u32[]{:S(2)}, u32[]{:S(2)}) %collective-permute-start.2) | collective-permute-done | bytes 65568 | tf_op jit(solution)/shard_map/ppermute | solution.py:133
  283.7 0.6 bitcast_subtract_fusion
  (75 shorter events, 5.9 us)
Async XLA Ops:
  7.2 18.8 %copy-start.15 = (s32[1,6]{1,0:T(1,128)S(1)}, s32[1,6]{1,0:T(1,128)}, u32[]{:S(2)}) copy-start(s32[1,6]{1,0:T(1,128)} %param.8) | copy-start | bytes 76
  7.2 19.6 %copy-start.14 = (s32[1,6]{1,0:T(1,128)S(1)}, s32[1,6]{1,0:T(1,128)}, u32[]{:S(2)}) copy-start(s32[1,6]{1,0:T(1,128)} %param.7) | copy-start | bytes 76
  7.2 112.5 %all-reduce.4.cloned.1.call-start = ((), (), s32[]{:S(2)}) async-start(), calls=%async_computation.2 | async-start | bytes 1048576 | tf_op jit(solution)/shard_map/psum | solution.py:106
  24.6 4.4 %collective-permute-start = (bf16[4,1024]{0,1:T(8,128)(2,1)S(1)}, bf16[4,1024]{0,1:T(8,128)(2,1)S(1)}, u32[]{:S(2)}, u32[]{:S(2)}) collective-permute-start(bf16[4,1024]{0,1:T(8,128)(2,1)S(1)} %slice.26), channel_id=1, source_target_pairs={{0,1},{1,2},{2,3},{3,4},{4,5},{5,6},{6,7},{8,9},{9,10},{10,11},{11... | collective-permute-start | bytes 24584 | tf_op jit(solution)/shard_map/ppermute | solution.py:21
  29.1 0.7 copy-start.10
  41.9 2.7 copy-start.8
  41.9 2.7 copy-start.9
  46.8 2.5 copy-start.3
  46.8 3.4 %copy-start.11 = (bf16[4,1024]{0,1:T(8,128)(2,1)S(1)}, bf16[4,1024]{0,1:T(8,128)(2,1)}, u32[]{:S(2)}) copy-start(bf16[4,1024]{0,1:T(8,128)(2,1)} %copy-done.10) | copy-start | bytes 24580
  56.9 2.8 copy-start
  61.3 121.9 %all-reduce.6.cloned.1.call-start = ((), (), s32[]{:S(2)}) async-start(), calls=%async_computation.3 | async-start | bytes 1048576 | tf_op jit(solution)/shard_map/psum | solution.py:106
  122.1 5.2 %copy-start.1 = (bf16[384,4096]{1,0:T(8,128)(2,1)S(1)}, bf16[384,4096]{1,0:T(8,128)(2,1)}, u32[]{:S(2)}) copy-start(bf16[384,4096]{1,0:T(8,128)(2,1)} %copy-done) | copy-start | bytes 9437188
  122.1 5.2 %copy-start.5 = (f32[1,32,4096]{2,1,0:T(8,128)S(1)}, f32[1,32,4096]{2,1,0:T(8,128)}, u32[]{:S(2)}) copy-start(f32[1,32,4096]{2,1,0:T(8,128)} %fusion.1) | copy-start | bytes 1572868
  122.2 5.2 %copy-start.7 = (f32[1,32,4096]{2,1,0:T(8,128)S(1)}, f32[1,32,4096]{2,1,0:T(8,128)}, u32[]{:S(2)}) copy-start(f32[1,32,4096]{2,1,0:T(8,128)} %all-reduce.4.cloned.1.call-done) | copy-start | bytes 1572868
  128.9 117.8 %all-reduce.8.cloned.1.call-start = ((), (), s32[]{:S(2)}) async-start(), calls=%async_computation.4 | async-start | bytes 1048576 | tf_op jit(solution)/shard_map/psum | solution.py:106
  185.7 5.2 %copy-start.2 = (bf16[384,4096]{1,0:T(8,128)(2,1)S(1)}, bf16[384,4096]{1,0:T(8,128)(2,1)}, u32[]{:S(2)}) copy-start(bf16[384,4096]{1,0:T(8,128)(2,1)} %copy-done) | copy-start | bytes 9437188
  185.7 5.2 %copy-start.4 = (f32[1,32,4096]{2,1,0:T(8,128)S(1)}, f32[1,32,4096]{2,1,0:T(8,128)}, u32[]{:S(2)}) copy-start(f32[1,32,4096]{2,1,0:T(8,128)} %fusion.7) | copy-start | bytes 1572868
  185.7 5.2 %copy-start.6 = (f32[1,32,4096]{2,1,0:T(8,128)S(1)}, f32[1,32,4096]{2,1,0:T(8,128)}, u32[]{:S(2)}) copy-start(f32[1,32,4096]{2,1,0:T(8,128)} %all-reduce.6.cloned.1.call-done) | copy-start | bytes 1572868
  190.4 2.1 copy-start.13
  192.5 79.9 %reduce-scatter.2.cloned.1.call-start = ((), (), s32[]{:S(2)}) async-start(), calls=%async_computation.5 | async-start | bytes 655360 | tf_op jit(solution)/shard_map/reduce_scatter | solution.py:119
  273.3 11.0 %copy-start.12 = (f32[32,1024]{1,0:T(8,128)}, f32[32,1024]{1,0:T(8,128)S(1)}, u32[]{:S(2)}) copy-start(f32[32,1024]{1,0:T(8,128)S(1)} %broadcast_divide_fusion) | copy-start | bytes 393220
  274.0 4.3 %collective-permute-start.1 = (f32[32,512]{1,0:T(8,128)S(1)}, f32[32,512]{1,0:T(8,128)S(1)}, u32[]{:S(2)}, u32[]{:S(2)}) collective-permute-start(f32[32,512]{1,0:T(8,128)S(1)} %fusion.36), channel_id=1, source_target_pairs={{0,8},{8,0},{16,24},{24,16},{1,9},{9,1},{17,25},{25,17},{2,10},{10... | collective-permute-start | bytes 196616 | tf_op jit(solution)/shard_map/ppermute | solution.py:133
  278.3 5.4 %collective-permute-start.2 = (f32[32,512]{1,0:T(8,128)S(1)}, f32[32,512]{1,0:T(8,128)S(1)}, u32[]{:S(2)}, u32[]{:S(2)}) collective-permute-start(f32[32,512]{1,0:T(8,128)S(1)} %add.410), channel_id=1, source_target_pairs={{0,16},{8,24},{16,0},{24,8},{1,17},{9,25},{17,1},{25,9},{2,18},{10... | collective-permute-start | bytes 196616 | tf_op jit(solution)/shard_map/ppermute | solution.py:133
Sparse Core Ops, SparseCore 0:
  61.4 58.2 all-reduce.3
  129.1 54.1 all-reduce.5
  192.6 54.0 all-reduce.7
  251.2 21.1 reduce-scatter.1
